TPU v7x, 32 devices: a whole 2x2x4 slice. The times are simulated.
32 devices in a mesh: seqa: 2 (over y), seqb: 4 (over z), tp: 4 (over x, core).
Axes of the slice: x: 2, y: 2, z: 4, core: 2. Of those that a mesh axis runs over, the one named last changes fastest.
Arguments:
- queries: bfloat16 [4096, 1024], P(('seqa', 'seqb'), 'tp'), may hold values from -6 to 6
- key_rows: bfloat16 [4096, 1024], P(('seqa', 'seqb'), 'tp'), may hold values from -6 to 6
- value_rows: bfloat16 [4096, 1024], P(('seqa', 'seqb'), 'tp'), may hold values from -6 to 6
- out_grad: bfloat16 [4096, 2048], P(('seqa', 'seqb'), 'tp'), may hold values from -6 to 6
- out_weight: bfloat16 [1024, 2048], P('tp'), may hold values from -0.1875 to 0.1875
- level_codes: int32 [4096, 160], P(('seqa', 'seqb'), 'tp'), may hold values from 0 to 7
Outputs:
- query_grad: bfloat16 [4096, 1024], P(('seqa', 'seqb'), 'tp')
- key_grad: bfloat16 [4096, 1024], P(('seqa', 'seqb'), 'tp')
- value_grad: bfloat16 [4096, 1024], P(('seqa', 'seqb'), 'tp')
All inputs are finite; a program needn't handle non-finite values.
Results may differ from a plain program's by a relative error of at most 0.0062.
Values may be sent and summed in bfloat16 or wider, within the bound.
A program may use at most 64 MiB of HBM per device.

v0:
```python
import math
import jax
import jax.numpy as jnp
from jax import lax
from jax.sharding import PartitionSpec as P

HEAD_DIM = 128


def swapped(x, axis, distance):
    return lax.ppermute(x, axis, [(i, i ^ 1 << distance) for i in range(lax.axis_size(axis))])


def per_device(queries, key_rows, value_rows, out_grad, out_weight, level_codes):
    shard_rows = queries.shape[0]
    head_count = out_weight.shape[0] // HEAD_DIM
    total_tokens = shard_rows * lax.axis_size(("seqa", "seqb"))
    scale_factor = 1.0 / math.sqrt(HEAD_DIM * total_tokens)
    head_grad = lax.dot_general(
        lax.all_gather(out_grad, "tp", axis=1, tiled=True),
        out_weight,
        (((1,), (1,)), ((), ())),
        preferred_element_type=jnp.float32,
    ).astype(jnp.bfloat16)
    level_weight = ((1 + level_codes).astype(jnp.float32) / 8.0).reshape(shard_rows, head_count, -1)
    shape_three = (shard_rows, head_count, HEAD_DIM)
    query_heads = queries.reshape(shape_three)
    key_head_matrix = key_rows.reshape(shape_three)
    value_head_matrix = value_rows.reshape(shape_three)
    grad_heads = head_grad.reshape(shape_three)
    level_top = shard_rows.bit_length() - 1
    span = min(shard_rows, 512)
    key_intra = jnp.zeros(shape_three, jnp.float32)
    value_intra = jnp.zeros(shape_three, jnp.float32)
    query_pos = jnp.arange(0, span, dtype=jnp.int32)[:, None]
    source_pos = jnp.arange(span, dtype=jnp.int32)[None, :]
    differ = jnp.bitwise_xor(query_pos, source_pos)
    level_map = jnp.zeros(differ.shape, jnp.int32)
    for bit_index in range(level_top):
        level_map = level_map + (differ >= 2**bit_index).astype(jnp.int32)
    causal = source_pos <= query_pos
    weight = jnp.zeros((head_count, span, span), jnp.float32)
    for level_index in range(level_top + 1):
        select = ((level_map == level_index) & causal).astype(jnp.float32)
        weight = weight + level_weight[:, :, level_index].T[:, :, None] * select[None]
    weight = weight * scale_factor
    scores = jnp.einsum(
        "thk,shk->hts", query_heads, key_head_matrix, preferred_element_type=jnp.float32
    )
    probs = (weight * scores).astype(jnp.bfloat16)
    dscore = jnp.einsum(
        "thv,shv->hts", grad_heads, value_head_matrix, preferred_element_type=jnp.float32
    )
    grad_mat = (weight * dscore).astype(jnp.bfloat16)
    query_parts = jnp.einsum(
        "hts,shk->thk", grad_mat, key_head_matrix, preferred_element_type=jnp.float32
    )
    key_intra = key_intra.at[:span].add(
        jnp.einsum("hts,thk->shk", grad_mat, query_heads, preferred_element_type=jnp.float32)
    )
    value_intra = value_intra.at[:span].add(
        jnp.einsum("hts,thv->shv", probs, grad_heads, preferred_element_type=jnp.float32)
    )
    carried_state = jnp.einsum(
        "ags,agr->gsr", key_head_matrix, value_head_matrix, preferred_element_type=jnp.float32
    )
    level_count = lax.axis_size(("seqa", "seqb")).bit_length() - 1
    device_index = lax.axis_index(("seqa", "seqb"))
    inter_weight = level_weight[:, :, level_top + 1 : level_top + 1 + level_count]
    scaled = (inter_weight[..., None] * grad_heads.astype(jnp.float32)[:, :, None, :]).astype(
        jnp.bfloat16
    )
    level_adjoint = scale_factor * jnp.einsum(
        "thk,thlv->lhkv", query_heads, scaled, preferred_element_type=jnp.float32
    )
    half_selector = [
        (device_index >> bit_index & 1).astype(jnp.float32) for bit_index in range(level_count)
    ]
    state_list = []
    total_adjoint = jnp.zeros(carried_state.shape, jnp.float32)
    for bit_index in range(level_count):
        upper = half_selector[bit_index]
        outgoing = upper * level_adjoint[bit_index] + (1.0 - upper) * carried_state
        received = swapped(outgoing, ("seqa", "seqb"), bit_index)
        for lower in range(bit_index):
            received = received + swapped(received, ("seqa", "seqb"), lower)
        state_list.append(received * upper)
        total_adjoint = total_adjoint + received * (1.0 - upper)
    level_states = jnp.stack(state_list, 0).astype(jnp.bfloat16)
    level_out = jnp.einsum(
        "thv,lhkv->thlk", grad_heads, level_states, preferred_element_type=jnp.float32
    )
    inter_sum = jnp.sum(inter_weight[..., None] * level_out, axis=2)
    adjoint_bfloat = total_adjoint.astype(jnp.bfloat16)
    query_grad = (query_parts + scale_factor * inter_sum).astype(jnp.bfloat16)
    key_grad = (
        key_intra
        + jnp.einsum(
            "ybe,bpe->ybp", value_head_matrix, adjoint_bfloat, preferred_element_type=jnp.float32
        )
    ).astype(jnp.bfloat16)
    value_grad = (
        value_intra
        + jnp.einsum(
            "mix,ixy->miy", key_head_matrix, adjoint_bfloat, preferred_element_type=jnp.float32
        )
    ).astype(jnp.bfloat16)
    flat = (shard_rows, head_count * HEAD_DIM)
    return (query_grad.reshape(flat), key_grad.reshape(flat), value_grad.reshape(flat))


def solution(mesh):
    placed = (
        P(("seqa", "seqb"), "tp"),
        P(("seqa", "seqb"), "tp"),
        P(("seqa", "seqb"), "tp"),
        P(("seqa", "seqb"), "tp"),
        P("tp", None),
        P(("seqa", "seqb"), "tp"),
    )
    return jax.shard_map(
        per_device,
        mesh=mesh,
        in_specs=placed,
        out_specs=(P(("seqa", "seqb"), "tp"), P(("seqa", "seqb"), "tp"), P(("seqa", "seqb"), "tp")),
        check_vma=False,
    )
```

profile of v0, /device:TPU:0, one launch (start us, length us, event | category | flops | bytes accessed | tf_op | source)
XLA Modules:
  0.0 76.9 jit_solution(2021714095588899248)
XLA Ops:
  7.9 0.9 %convert_multiply_fusion = f32[512,40]{0,1:T(8,128)S(1)} fusion(s32[512,40]{0,1:T(8,128)} %param.19), kind=kLoop, calls=%fused_computation.91 | loop fusion | flops 61440 | bytes 163840 | tf_op jit(solution)/shard_map/div | solution.py:25
  8.9 1.8 %fusion.35 = (f32[512,512]{1,0:T(8,128)}, f32[512,512]{1,0:T(8,128)}) fusion(), kind=kLoop, calls=%fused_computation.49 | loop fusion | flops 8912896 | bytes 2097152 | tf_op jit(solution)/shard_map/convert_element_type | solution.py:44
  10.6 1.9 %fusion.33 = (f32[512,512]{1,0:T(8,128)}, f32[512,512]{1,0:T(8,128)}) fusion(), kind=kLoop, calls=%fused_computation.47 | loop fusion | flops 8912896 | bytes 2097152 | tf_op jit(solution)/shard_map/convert_element_type | solution.py:44
  12.5 1.8 %fusion.31 = (f32[512,512]{1,0:T(8,128)}, f32[512,512]{1,0:T(8,128)}) fusion(), kind=kLoop, calls=%fused_computation.45 | loop fusion | flops 8912896 | bytes 2097152 | tf_op jit(solution)/shard_map/convert_element_type | solution.py:44
  14.4 1.8 %fusion.29 = (f32[512,512]{1,0:T(8,128)}, f32[512,512]{1,0:T(8,128)}) fusion(), kind=kLoop, calls=%fused_computation.43 | loop fusion | flops 8912896 | bytes 2097152 | tf_op jit(solution)/shard_map/convert_element_type | solution.py:44
  16.2 1.8 %fusion.27 = (f32[512,512]{1,0:T(8,128)}, f32[512,512]{1,0:T(8,128)}) fusion(), kind=kLoop, calls=%fused_computation.41 | loop fusion | flops 8912896 | bytes 2097152 | tf_op jit(solution)/shard_map/convert_element_type | solution.py:44
  18.0 16.8 %all-gather.2.cloned.1.call-done = bf16[512,2048]{1,0:T(8,128)(2,1)} async-done(((bf16[512,512]{1,0:T(8,128)(2,1)}), bf16[512,2048]{1,0:T(8,128)(2,1)}) %all-gather.2.cloned.1.call-update) | async-done | bytes 2097168 | tf_op jit(solution)/shard_map/all_gather | solution.py:20
  34.9 2.5 %convolution_convert_fusion = bf16[512,256]{0,1:T(8,128)(2,1)S(1)} fusion(bf16[512,2048]{1,0:T(8,128)(2,1)} %all-gather.2.cloned.1.call-done, bf16[256,2048]{1,0:T(8,128)(2,1)S(1)} %copy-done), kind=kOutput, calls=%fused_computation.15 | convolution fusion | flops 537001984 | bytes 3407872 | tf_op jit(solution)/shard_map/dot_general | solution.py:19
  37.9 0.9 %fusion.71 = (f32[2,128,128]{1,2,0:T(8,128)}, f32[2,128,128]{1,2,0:T(8,128)S(1)}, f32[2,128,128]{1,2,0:T(8,128)S(1)}) fusion(f32[3,2,128,128]{2,3,0,1:T(8,128)S(1)} %fusion.7, f32[]{:T(128)S(6)} %sub.12, f32[]{:T(128)S(6)} %convert_element_type.607, f32[]{:T(128)S(6)} %sub.14, f32[]{:T(128)S(6)} %convert_element_type.611, f32[]{:T(128)S(6)} %sub.13, ...), kind=kOutput, calls=%fused_computation.86 | convolution fusion | flops 33849344 | bytes 1310744 | tf_op jit(solution)/shard_map/ags,agr->gsr/dot_general | solution.py:64
  38.9 1.5 %collective-permute-start.3 = (f32[2,128,128]{1,2,0:T(8,128)S(1)}, f32[2,128,128]{1,2,0:T(8,128)S(1)}, u32[]{:S(2)}, u32[]{:S(2)}) collective-permute-start(f32[2,128,128]{1,2,0:T(8,128)S(1)} %get-tuple-element.50), channel_id=1, source_target_pairs={{0,16},{4,20},{8,24},{12,28},{16,0},{20,4},{24,8},{28,12},{1,17},{... | collective-permute-start | bytes 393224 | tf_op jit(solution)/shard_map/ppermute | solution.py:11
  40.4 3.5 %add_multiply_fusion = f32[2,512,512]{2,1,0:T(8,128)S(1)} fusion(f32[512,512]{1,0:T(8,128)S(1)} %copy-done.3, f32[2,512]{1,0:T(2,128)S(1)} %get-tuple-element.66, f32[512,512]{1,0:T(8,128)S(1)} %copy-done.2, f32[2,512]{1,0:T(2,128)S(1)} %get-tuple-element.67, f32[512,512]{1,0:T(8,128)S(1)} %copy-done.5, f32[2,512]{1,0:T(2,128)S(1)} %get-tuple-element.68, ...), kind=kLoop, calls=%fused_computation.2 | loop fusion | flops 10485760 | bytes 12623872 | tf_op jit(solution)/shard_map/mul | solution.py:46
  43.9 2.5 %collective-permute-start.1 = (f32[2,128,128]{1,2,0:T(8,128)S(1)}, f32[2,128,128]{1,2,0:T(8,128)}, u32[]{:S(2)}, u32[]{:S(2)}) collective-permute-start(f32[2,128,128]{1,2,0:T(8,128)S(1)} %get-tuple-element.51), channel_id=1, source_target_pairs={{0,8},{4,12},{8,0},{12,4},{16,24},{20,28},{24,16},{28,20},{1,9},{5... | collective-permute-start | bytes 393224 | tf_op jit(solution)/shard_map/ppermute | solution.py:11
  46.4 1.5 %collective-permute-start.4 = (f32[2,128,128]{1,2,0:T(8,128)S(1)}, f32[2,128,128]{1,2,0:T(8,128)S(1)}, u32[]{:S(2)}, u32[]{:S(2)}) collective-permute-start(f32[2,128,128]{1,2,0:T(8,128)S(1)} %collective-permute-done.3), channel_id=1, source_target_pairs={{0,4},{4,0},{8,12},{12,8},{16,20},{20,16},{24,28},{28,24},{1,5},{5... | collective-permute-start | bytes 393224 | tf_op jit(solution)/shard_map/ppermute | solution.py:11
  47.9 1.5 %multiply_convert_fusion.1 = bf16[2,512,512]{2,1,0:T(8,128)(2,1)} fusion(f32[2,512,512]{2,1,0:T(8,128)S(1)} %add_multiply_fusion, bf16[512,2,128]{0,2,1:T(8,128)(2,1)S(1)} %bitcast.185, bf16[512,256]{1,0:T(8,128)(2,1)S(1)} %copy-done.14), kind=kOutput, calls=%fused_computation.1 | convolution fusion | flops 135266304 | bytes 3670016 | tf_op jit(solution)/shard_map/thv,shv->hts/dot_general | solution.py:51
  49.9 3.4 %collective-permute-done.1 = f32[2,128,128]{1,2,0:T(8,128)} collective-permute-done((f32[2,128,128]{1,2,0:T(8,128)S(1)}, f32[2,128,128]{1,2,0:T(8,128)}, u32[]{:S(2)}, u32[]{:S(2)}) %collective-permute-start.1) | collective-permute-done | bytes 131104 | tf_op jit(solution)/shard_map/ppermute | solution.py:11
  53.8 3.4 %collective-permute-start.5 = (f32[2,128,128]{1,2,0:T(8,128)S(1)}, f32[2,128,128]{1,2,0:T(8,128)}, u32[]{:S(2)}, u32[]{:S(2)}) collective-permute-start(f32[2,128,128]{1,2,0:T(8,128)S(1)} %add.524), channel_id=1, source_target_pairs={{0,8},{4,12},{8,0},{12,4},{16,24},{20,28},{24,16},{28,20},{1,9},{5... | collective-permute-start | bytes 393224 | tf_op jit(solution)/shard_map/ppermute | solution.py:11
  57.2 2.4 %fusion.1 = f32[2,128,512]{2,1,0:T(8,128)} fusion(bf16[512,2,128]{0,2,1:T(8,128)(2,1)S(1)} %bitcast.186, f32[2,512,512]{2,1,0:T(8,128)S(1)} %add_multiply_fusion, bf16[512,256]{1,0:T(8,128)(2,1)} %param.14, bf16[512,256]{1,0:T(8,128)(2,1)} %param.15), kind=kOutput, calls=%fused_computation.6 | convolution fusion | flops 269484032 | bytes 3407872 | tf_op jit(solution)/shard_map/hts,thv->shv/dot_general | solution.py:62
  59.6 2.0 %collective-permute-done.2 = f32[2,128,128]{1,2,0:T(8,128)} collective-permute-done((f32[2,128,128]{1,2,0:T(8,128)}, f32[2,128,128]{1,2,0:T(8,128)}, u32[]{:S(2)}, u32[]{:S(2)}) %collective-permute-start.2) | collective-permute-done | bytes 131104 | tf_op jit(solution)/shard_map/ppermute | solution.py:11
  61.7 1.9 %collective-permute-done.5 = f32[2,128,128]{1,2,0:T(8,128)} collective-permute-done((f32[2,128,128]{1,2,0:T(8,128)S(1)}, f32[2,128,128]{1,2,0:T(8,128)}, u32[]{:S(2)}, u32[]{:S(2)}) %collective-permute-start.5) | collective-permute-done | bytes 131104 | tf_op jit(solution)/shard_map/ppermute | solution.py:11
  63.5 1.2 %add_convert_fusion = (bf16[2,128,128]{1,2,0:T(8,128)(2,1)S(1)}, bf16[1,2,128,128]{2,3,1,0:T(8,128)(2,1)S(1)}, bf16[1,2,128,128]{2,3,1,0:T(8,128)(2,1)S(1)}, bf16[1,2,128,128]{2,3,1,0:T(8,128)(2,1)S(1)}) fusion(f32[2,128,128]{1,2,0:T(8,128)} %collective-permute-done, f32[]{:T(128)S(6)} %sub.14, f32[]{:T(128)S(6)} %sub.13, f32[]{:T(128)S(6)} %sub.12, ...), kind=kLoop, calls=%fused_computation.87 | loop fusion | flops 458752 | bytes 917528 | tf_op jit(solution)/shard_map/convert_element_type | solution.py:94
  65.7 0.8 %copy.56 = bf16[512,256]{1,0:T(8,128)(2,1)} copy(bf16[512,256]{0,1:T(8,128)(2,1)S(1)} %bitcast.190) | data formatting | bytes 524288
  66.8 1.3 %fusion.5 = bf16[512,2,128]{0,2,1:T(8,128)(2,1)S(1)} fusion(f32[512,2,128]{0,2,1:T(8,128)S(1)} %convolution_bitcast_fusion.1, bf16[2,512,512]{2,1,0:T(8,128)(2,1)S(1)} %copy-done.1, bf16[512,256]{1,0:T(8,128)(2,1)} %param.14), kind=kOutput, calls=%fused_computation.14 | convolution fusion | flops 134479872 | bytes 2097152 | tf_op jit(solution)/shard_map/hts,thk->shk/dot_general | solution.py:59
  68.1 0.8 %copy.57 = bf16[512,256]{1,0:T(8,128)(2,1)} copy(bf16[512,256]{0,1:T(8,128)(2,1)S(1)} %bitcast.189) | data formatting | bytes 524288
  69.2 0.8 %copy.58 = bf16[512,256]{1,0:T(8,128)(2,1)} copy(bf16[512,256]{0,1:T(8,128)(2,1)S(1)} %bitcast.188) | data formatting | bytes 524288
  (58 shorter events, 3.8 us)
Async XLA Ops:
  7.2 27.7 %copy-start = (bf16[256,2048]{1,0:T(8,128)(2,1)S(1)}, bf16[256,2048]{1,0:T(8,128)(2,1)}, u32[]{:S(2)}) copy-start(bf16[256,2048]{1,0:T(8,128)(2,1)} %param.18) | copy-start | bytes 3145732
  7.2 27.7 %all-gather.2.cloned.1.call-start = ((), (), s32[]{:S(2)}) async-start(), calls=%async_computation | async-start | bytes 2621440 | tf_op jit(solution)/shard_map/all_gather | solution.py:20
  16.2 21.3 %copy-start.16 = (bf16[512,256]{1,0:T(8,128)(2,1)S(1)}, bf16[512,256]{1,0:T(8,128)(2,1)}, u32[]{:S(2)}) copy-start(bf16[512,256]{1,0:T(8,128)(2,1)} %param.14) | copy-start | bytes 786436
  16.2 21.7 %copy-start.13 = (bf16[512,256]{1,0:T(8,128)(2,1)S(1)}, bf16[512,256]{1,0:T(8,128)(2,1)}, u32[]{:S(2)}) copy-start(bf16[512,256]{1,0:T(8,128)(2,1)} %param.16) | copy-start | bytes 786436
  34.9 3.0 %copy-start.10 = (bf16[512,256]{1,0:T(8,128)(2,1)S(1)}, bf16[512,256]{1,0:T(8,128)(2,1)}, u32[]{:S(2)}) copy-start(bf16[512,256]{1,0:T(8,128)(2,1)} %param.15) | copy-start | bytes 786436
  34.9 5.5 %copy-start.5 = (f32[512,512]{1,0:T(8,128)S(1)}, f32[512,512]{1,0:T(8,128)}, u32[]{:S(2)}) copy-start(f32[512,512]{1,0:T(8,128)} %get-tuple-element.83) | copy-start | bytes 3145732
  34.9 5.5 %copy-start.6 = (f32[512,512]{1,0:T(8,128)S(1)}, f32[512,512]{1,0:T(8,128)}, u32[]{:S(2)}) copy-start(f32[512,512]{1,0:T(8,128)} %get-tuple-element.80) | copy-start | bytes 3145732
  34.9 5.5 %copy-start.7 = (f32[512,512]{1,0:T(8,128)S(1)}, f32[512,512]{1,0:T(8,128)}, u32[]{:S(2)}) copy-start(f32[512,512]{1,0:T(8,128)} %get-tuple-element.81) | copy-start | bytes 3145732
  34.9 5.4 %copy-start.8 = (f32[512,512]{1,0:T(8,128)S(1)}, f32[512,512]{1,0:T(8,128)}, u32[]{:S(2)}) copy-start(f32[512,512]{1,0:T(8,128)} %get-tuple-element.78) | copy-start | bytes 3145732
  34.9 5.4 %copy-start.9 = (f32[512,512]{1,0:T(8,128)S(1)}, f32[512,512]{1,0:T(8,128)}, u32[]{:S(2)}) copy-start(f32[512,512]{1,0:T(8,128)} %get-tuple-element.79) | copy-start | bytes 3145732
  37.4 2.9 %copy-start.2 = (f32[512,512]{1,0:T(8,128)S(1)}, f32[512,512]{1,0:T(8,128)}, u32[]{:S(2)}) copy-start(f32[512,512]{1,0:T(8,128)} %get-tuple-element.84) | copy-start | bytes 3145732
  37.4 2.9 %copy-start.3 = (f32[512,512]{1,0:T(8,128)S(1)}, f32[512,512]{1,0:T(8,128)}, u32[]{:S(2)}) copy-start(f32[512,512]{1,0:T(8,128)} %get-tuple-element.85) | copy-start | bytes 3145732
  37.4 2.9 %copy-start.4 = (f32[512,512]{1,0:T(8,128)S(1)}, f32[512,512]{1,0:T(8,128)}, u32[]{:S(2)}) copy-start(f32[512,512]{1,0:T(8,128)} %get-tuple-element.82) | copy-start | bytes 3145732
  38.9 7.5 %collective-permute-start.3 = (f32[2,128,128]{1,2,0:T(8,128)S(1)}, f32[2,128,128]{1,2,0:T(8,128)S(1)}, u32[]{:S(2)}, u32[]{:S(2)}) collective-permute-start(f32[2,128,128]{1,2,0:T(8,128)S(1)} %get-tuple-element.50), channel_id=1, source_target_pairs={{0,16},{4,20},{8,24},{12,28},{16,0},{20,4},{24,8},{28,12},{1,17},{... | collective-permute-start | bytes 393224 | tf_op jit(solution)/shard_map/ppermute | solution.py:11
  40.4 7.5 %copy-start.14 = (bf16[512,256]{1,0:T(8,128)(2,1)S(1)}, bf16[512,256]{1,0:T(8,128)(2,1)}, u32[]{:S(2)}) copy-start(bf16[512,256]{1,0:T(8,128)(2,1)} %param.16) | copy-start | bytes 786436
  43.9 9.3 %collective-permute-start.1 = (f32[2,128,128]{1,2,0:T(8,128)S(1)}, f32[2,128,128]{1,2,0:T(8,128)}, u32[]{:S(2)}, u32[]{:S(2)}) collective-permute-start(f32[2,128,128]{1,2,0:T(8,128)S(1)} %get-tuple-element.51), channel_id=1, source_target_pairs={{0,8},{4,12},{8,0},{12,4},{16,24},{20,28},{24,16},{28,20},{1,9},{5... | collective-permute-start | bytes 393224 | tf_op jit(solution)/shard_map/ppermute | solution.py:11
  46.4 7.4 %collective-permute-start.4 = (f32[2,128,128]{1,2,0:T(8,128)S(1)}, f32[2,128,128]{1,2,0:T(8,128)S(1)}, u32[]{:S(2)}, u32[]{:S(2)}) collective-permute-start(f32[2,128,128]{1,2,0:T(8,128)S(1)} %collective-permute-done.3), channel_id=1, source_target_pairs={{0,4},{4,0},{8,12},{12,8},{16,20},{20,16},{24,28},{28,24},{1,5},{5... | collective-permute-start | bytes 393224 | tf_op jit(solution)/shard_map/ppermute | solution.py:11
  49.4 10.3 %collective-permute-start = (f32[2,128,128]{1,2,0:T(8,128)}, f32[2,128,128]{1,2,0:T(8,128)}, u32[]{:S(2)}, u32[]{:S(2)}) collective-permute-start(f32[2,128,128]{1,2,0:T(8,128)} %get-tuple-element.49), channel_id=1, source_target_pairs={{0,4},{4,0},{8,12},{12,8},{16,20},{20,16},{24,28},{28,24},{1,5},{5... | collective-permute-start | bytes 393224 | tf_op jit(solution)/shard_map/ppermute | solution.py:11
  53.3 8.4 %collective-permute-start.2 = (f32[2,128,128]{1,2,0:T(8,128)}, f32[2,128,128]{1,2,0:T(8,128)}, u32[]{:S(2)}, u32[]{:S(2)}) collective-permute-start(f32[2,128,128]{1,2,0:T(8,128)} %collective-permute-done.1), channel_id=1, source_target_pairs={{0,4},{4,0},{8,12},{12,8},{16,20},{20,16},{24,28},{28,24},{1,5},{5... | collective-permute-start | bytes 393224 | tf_op jit(solution)/shard_map/ppermute | solution.py:11
  53.8 7.9 %copy-start.17 = (f32[2,128,128]{1,2,0:T(8,128)}, f32[2,128,128]{1,2,0:T(8,128)S(1)}, u32[]{:S(2)}) copy-start(f32[2,128,128]{1,2,0:T(8,128)S(1)} %add.524) | copy-start | bytes 393220
  53.8 9.7 %collective-permute-start.5 = (f32[2,128,128]{1,2,0:T(8,128)S(1)}, f32[2,128,128]{1,2,0:T(8,128)}, u32[]{:S(2)}, u32[]{:S(2)}) collective-permute-start(f32[2,128,128]{1,2,0:T(8,128)S(1)} %add.524), channel_id=1, source_target_pairs={{0,8},{4,12},{8,0},{12,4},{16,24},{20,28},{24,16},{28,20},{1,9},{5... | collective-permute-start | bytes 393224 | tf_op jit(solution)/shard_map/ppermute | solution.py:11
  59.6 5.6 %copy-start.1 = (bf16[2,512,512]{2,1,0:T(8,128)(2,1)S(1)}, bf16[2,512,512]{2,1,0:T(8,128)(2,1)}, u32[]{:S(2)}) copy-start(bf16[2,512,512]{2,1,0:T(8,128)(2,1)} %multiply_convert_fusion.1) | copy-start | bytes 3145732
  59.6 5.6 %copy-start.11 = (bf16[512,256]{1,0:T(8,128)(2,1)S(1)}, bf16[512,256]{1,0:T(8,128)(2,1)}, u32[]{:S(2)}) copy-start(bf16[512,256]{1,0:T(8,128)(2,1)} %param.15) | copy-start | bytes 786436
  65.7 3.3 %copy-start.12 = (f32[2,128,512]{2,1,0:T(8,128)S(1)}, f32[2,128,512]{2,1,0:T(8,128)}, u32[]{:S(2)}) copy-start(f32[2,128,512]{2,1,0:T(8,128)} %fusion.1) | copy-start | bytes 1572868
  (1 other events, 1.8 us)
Sparse Core Ops, SparseCore 0:
  9.5 25.2 all-gather.1
where the time goes:
time: 77.2 us; the launch traced here: 76.9 us
  waiting for transfers between devices  25 us (32%)
  other arithmetic  14.8 us (19%)
  between operations  14.4 us (19%)
  matrix products  10.4 us (13%)
  starting transfers between devices  9.74 us (13%)
  local copies, waits for them, and re-layouts  2.68 us (3%)
    all_gather x1, waiting for transfers between devices, per_device(): lax.all_gather(out_grad, 'tp', axis=1, tiled=True)  16.8 us
    ppermute x6, starting transfers between devices, swapped(): lax.ppermute(x, axis, [(i, i ^ 1 << distance) for i in range(lax.axis_siz...  9.7 us
    convert_element_type x5, other arithmetic, per_device(): select = ((level_map == level_index) & causal).astype(jnp.float32)  9.07 us
    ppermute x6, waiting for transfers between devices, swapped(): lax.ppermute(x, axis, [(i, i ^ 1 << distance) for i in range(lax.axis_siz...  7.45 us
    mul x1, other arithmetic, per_device(): weight = weight * scale_factor  3.52 us
    unnamed x39, local copies, waits for them, and re-layouts  2.61 us
    dot_general x1, matrix products, per_device(): lax.dot_general(lax.all_gather(out_grad, 'tp', axis=1, tiled=True), out_w...  2.49 us
    dot_general x1, matrix products, per_device(): jnp.einsum('hts,thv->shv', probs, grad_heads, preferred_element_type=jnp....  2.4 us
  transfers between devices with their start and end apart: 7, of which 5 were waited for; matrix products, arithmetic and copies ran while one was open for 23% of the time, Pallas kernels for 0%

commit v1 on v0

--- a/solution.py
+++ b/solution.py
@@ -1,3 +1,4 @@
+import functools
 import math
 import jax
 import jax.numpy as jnp
@@ -5,6 +6,26 @@
 from jax.sharding import PartitionSpec as P
 
 HEAD_DIM = 128
+
+
+def records_put(load, along_axis, array_dim):
+    nd = lax.axis_size(along_axis)
+    found = tuple(((j0, (j0 + 1) % nd) for j0 in range(nd)))
+    nodes = tuple(((j0, (j0 - 1) % nd) for j0 in range(nd)))
+    arr_next, spare = ([load], [load])
+    for _ in range(nd // 2):
+        passed = lax.ppermute(arr_next[-1], along_axis, found)
+        arr_next.append(passed)
+    for _ in tuple(range((nd - 1) // 2)):
+        local_out = lax.ppermute(spare[-1], along_axis, nodes)
+        spare.append(local_out)
+    mixed_arr = jnp.concatenate([*arr_next[::-1], *spare[1:]], axis=array_dim)
+    tmp = lax.axis_index(along_axis)
+    step_out = jnp.roll(mixed_arr, shift=(tmp - nd // 2) * load.shape[array_dim], axis=array_dim)
+    return step_out
+
+
+shape_the_lines = functools.partial(records_put, along_axis="tp", array_dim=1)
 
 
 def swapped(x, axis, distance):
@@ -17,7 +38,7 @@
     total_tokens = shard_rows * lax.axis_size(("seqa", "seqb"))
     scale_factor = 1.0 / math.sqrt(HEAD_DIM * total_tokens)
     head_grad = lax.dot_general(
-        lax.all_gather(out_grad, "tp", axis=1, tiled=True),
+        shape_the_lines(out_grad),
         out_weight,
         (((1,), (1,)), ((), ())),
         preferred_element_type=jnp.float32,

time: 77.2 us -> 56 us (0.73)
  between operations: 14.4 us -> 1.04 us
  waiting for transfers between devices: 25 us -> 17.8 us
  starting transfers between devices: 9.74 us -> 15.7 us
  other arithmetic: 14.8 us -> 9.35 us
  matrix products: 10.4 us -> 8.66 us
    all_gather x1 -> x0, waiting for transfers between devices: 16.8 us -> none  [per_device(): lax.all_gather(out_grad, 'tp', axis=1, tiled=True)]
    ppermute x0 -> x3, waiting for transfers between devices: none -> 9.62 us  [the longest x2 9.61 us: records_put(): passed = lax.ppermute(arr_next[-1], along_axis, found)]
    ppermute x0 -> x3, starting transfers between devices: none -> 5.08 us  [the longest x2 3.1 us: records_put(): passed = lax.ppermute(arr_next[-1], along_axis, found)]
    convert_element_type x5, other arithmetic: 9.07 us -> 6.3 us  [per_device(): select = ((level_map == level_index) & causal).astype(jnp.float32)]
    dot_general x1, matrix products: 2.49 us -> 0.77 us  [per_device(): lax.dot_general(shape_the_lines(out_grad), out_weight, (((1,), (1,)), (()...]
    mul x1, other arithmetic: 3.52 us -> 1.81 us  [per_device(): weight = weight * scale_factor]
    ppermute x6, starting transfers between devices: 9.7 us -> 10.7 us  [swapped(): lax.ppermute(x, axis, [(i, i ^ 1 << distance) for i in range(lax.axis_siz...]
    div x1, other arithmetic: 0.9 us -> 0.01 us  [per_device(): (1 + level_codes).astype(jnp.float32) / 8.0]
  transfers between devices with their start and end apart: 7 -> 9, of which waited for: 5 -> 6; matrix products, arithmetic and copies ran while one was open for 23% -> 22% of each run, Pallas kernels for 0% -> 0%
where the time goes in v1:
time: 56 us; the launch traced here: 55.8 us
  waiting for transfers between devices  17.8 us (32%)
  starting transfers between devices  15.7 us (28%)
  other arithmetic  9.35 us (17%)
  matrix products  8.66 us (15%)
  local copies, waits for them, and re-layouts  3.25 us (6%)
  between operations  1.04 us (2%)
    ppermute x6, starting transfers between devices, swapped(): lax.ppermute(x, axis, [(i, i ^ 1 << distance) for i in range(lax.axis_siz...  10.7 us
    ppermute x2, waiting for transfers between devices, records_put(): passed = lax.ppermute(arr_next[-1], along_axis, found)  9.61 us
    ppermute x6, waiting for transfers between devices, swapped(): lax.ppermute(x, axis, [(i, i ^ 1 << distance) for i in range(lax.axis_siz...  8.18 us
    convert_element_type x5, other arithmetic, per_device(): select = ((level_map == level_index) & causal).astype(jnp.float32)  6.3 us
    unnamed x42, local copies, waits for them, and re-layouts  3.1 us
    ppermute x2, starting transfers between devices, records_put(): passed = lax.ppermute(arr_next[-1], along_axis, found)  3.1 us
    dot_general x1, matrix products, per_device(): jnp.einsum('hts,thv->shv', probs, grad_heads, preferred_element_type=jnp....  2.4 us
    ppermute x1, starting transfers between devices, records_put(): local_out = lax.ppermute(spare[-1], along_axis, nodes)  1.98 us
  transfers between devices with their start and end apart: 9, of which 6 were waited for; matrix products, arithmetic and copies ran while one was open for 22% of the time, Pallas kernels for 0%

profile of v1, /device:TPU:0, one launch (start us, length us, event | category | flops | bytes accessed | tf_op | source)
XLA Modules:
  0.0 55.8 jit_solution(14474551424669789795)
XLA Ops:
  1.2 2.0 %collective-permute-start.2 = (bf16[512,512]{1,0:T(8,128)(2,1)}, bf16[512,512]{1,0:T(8,128)(2,1)S(1)}, u32[]{:S(2)}, u32[]{:S(2)}) collective-permute-start(bf16[512,512]{1,0:T(8,128)(2,1)} %param.17), channel_id=1, source_target_pairs={{0,3},{1,0},{2,1},{3,2},{4,7},{5,4},{6,5},{7,6},{8,11},{9,8},{10,9... | collective-permute-start | bytes 1572872 | tf_op jit(solution)/shard_map/ppermute | solution.py:20
  3.2 1.8 %fusion.40 = (f32[512,512]{1,0:T(8,128)}, f32[512,512]{1,0:T(8,128)}) fusion(), kind=kLoop, calls=%fused_computation.51 | loop fusion | flops 8912896 | bytes 2097152 | tf_op jit(solution)/shard_map/convert_element_type | solution.py:65
  5.0 1.8 %fusion.38 = (f32[512,512]{1,0:T(8,128)}, f32[512,512]{1,0:T(8,128)}) fusion(), kind=kLoop, calls=%fused_computation.49 | loop fusion | flops 8912896 | bytes 2097152 | tf_op jit(solution)/shard_map/convert_element_type | solution.py:65
  6.9 1.8 %fusion.36 = (f32[512,512]{1,0:T(8,128)}, f32[512,512]{1,0:T(8,128)}) fusion(), kind=kLoop, calls=%fused_computation.47 | loop fusion | flops 8912896 | bytes 2097152 | tf_op jit(solution)/shard_map/convert_element_type | solution.py:65
  8.7 4.5 %collective-permute-done = bf16[512,512]{1,0:T(8,128)(2,1)S(1)} collective-permute-done((bf16[512,512]{1,0:T(8,128)(2,1)}, bf16[512,512]{1,0:T(8,128)(2,1)S(1)}, u32[]{:S(2)}, u32[]{:S(2)}) %collective-permute-start) | collective-permute-done | bytes 524320 | tf_op jit(solution)/shard_map/ppermute | solution.py:17
  13.2 2.6 %collective-permute-start.1 = (bf16[512,512]{1,0:T(8,128)(2,1)S(1)}, bf16[512,512]{1,0:T(8,128)(2,1)S(1)}, u32[]{:S(2)}, u32[]{:S(2)}) collective-permute-start(bf16[512,512]{1,0:T(8,128)(2,1)S(1)} %collective-permute-done), channel_id=1, source_target_pairs={{0,1},{1,2},{2,3},{3,0},{4,5},{5,6},{6,7},{7,4},{8,9},{9,10},{10,1... | collective-permute-start | bytes 1572872 | tf_op jit(solution)/shard_map/ppermute | solution.py:17
  16.7 5.1 %collective-permute-done.1 = bf16[512,512]{1,0:T(8,128)(2,1)S(1)} collective-permute-done((bf16[512,512]{1,0:T(8,128)(2,1)S(1)}, bf16[512,512]{1,0:T(8,128)(2,1)S(1)}, u32[]{:S(2)}, u32[]{:S(2)}) %collective-permute-start.1) | collective-permute-done | bytes 524320 | tf_op jit(solution)/shard_map/ppermute | solution.py:17
  23.8 0.9 %fusion.76 = (f32[2,128,128]{1,2,0:T(8,128)}, f32[2,128,128]{1,2,0:T(8,128)S(1)}, f32[2,128,128]{1,2,0:T(8,128)S(1)}) fusion(f32[3,2,128,128]{2,3,0,1:T(8,128)S(1)} %fusion.12, f32[]{:T(128)S(6)} %sub.21, f32[]{:T(128)S(6)} %convert_element_type.607, f32[]{:T(128)S(6)} %sub.23, f32[]{:T(128)S(6)} %convert_element_type.611, f32[]{:T(128)S(6)} %sub.22, ...), kind=kOutput, calls=%fused_computation.88 | convolution fusion | flops 33849344 | bytes 1310744 | tf_op jit(solution)/shard_map/ags,agr->gsr/dot_general | solution.py:85
  24.8 3.1 %collective-permute-start.6 = (f32[2,128,128]{1,2,0:T(8,128)S(1)}, f32[2,128,128]{1,2,0:T(8,128)S(1)}, u32[]{:S(2)}, u32[]{:S(2)}) collective-permute-start(f32[2,128,128]{1,2,0:T(8,128)S(1)} %get-tuple-element.50), channel_id=1, source_target_pairs={{0,16},{4,20},{8,24},{12,28},{16,0},{20,4},{24,8},{28,12},{1,17},{... | collective-permute-start | bytes 393224 | tf_op jit(solution)/shard_map/ppermute | solution.py:32
  27.9 1.8 %add_multiply_fusion = f32[2,512,512]{2,1,0:T(8,128)S(1)} fusion(f32[512,512]{1,0:T(8,128)S(1)} %copy-done.3, f32[2,512]{1,0:T(2,128)S(1)} %get-tuple-element.66, f32[512,512]{1,0:T(8,128)S(1)} %copy-done.2, f32[2,512]{1,0:T(2,128)S(1)} %get-tuple-element.67, f32[512,512]{1,0:T(8,128)S(1)} %copy-done.5, f32[2,512]{1,0:T(2,128)S(1)} %get-tuple-element.68, ...), kind=kLoop, calls=%fused_computation.4 | loop fusion | flops 10485760 | bytes 12623872 | tf_op jit(solution)/shard_map/mul | solution.py:67
  29.8 2.7 %collective-permute-start.4 = (f32[2,128,128]{1,2,0:T(8,128)S(1)}, f32[2,128,128]{1,2,0:T(8,128)}, u32[]{:S(2)}, u32[]{:S(2)}) collective-permute-start(f32[2,128,128]{1,2,0:T(8,128)S(1)} %get-tuple-element.51), channel_id=1, source_target_pairs={{0,8},{4,12},{8,0},{12,4},{16,24},{20,28},{24,16},{28,20},{1,9},{5... | collective-permute-start | bytes 393224 | tf_op jit(solution)/shard_map/ppermute | solution.py:32
  32.4 1.6 %collective-permute-start.7 = (f32[2,128,128]{1,2,0:T(8,128)S(1)}, f32[2,128,128]{1,2,0:T(8,128)S(1)}, u32[]{:S(2)}, u32[]{:S(2)}) collective-permute-start(f32[2,128,128]{1,2,0:T(8,128)S(1)} %collective-permute-done.6), channel_id=1, source_target_pairs={{0,4},{4,0},{8,12},{12,8},{16,20},{20,16},{24,28},{28,24},{1,5},{5... | collective-permute-start | bytes 393224 | tf_op jit(solution)/shard_map/ppermute | solution.py:32
  34.0 1.5 %multiply_convert_fusion.1 = bf16[2,512,512]{2,1,0:T(8,128)(2,1)} fusion(f32[2,512,512]{2,1,0:T(8,128)S(1)} %add_multiply_fusion, bf16[512,2,128]{0,2,1:T(8,128)(2,1)S(1)} %bitcast.184, bf16[512,256]{1,0:T(8,128)(2,1)S(1)} %copy-done.12), kind=kOutput, calls=%fused_computation.1 | convolution fusion | flops 135266304 | bytes 3670016 | tf_op jit(solution)/shard_map/thv,shv->hts/dot_general | solution.py:72
  35.9 3.4 %collective-permute-done.4 = f32[2,128,128]{1,2,0:T(8,128)} collective-permute-done((f32[2,128,128]{1,2,0:T(8,128)S(1)}, f32[2,128,128]{1,2,0:T(8,128)}, u32[]{:S(2)}, u32[]{:S(2)}) %collective-permute-start.4) | collective-permute-done | bytes 131104 | tf_op jit(solution)/shard_map/ppermute | solution.py:32
  39.5 0.9 %collective-permute-done.7 = f32[2,128,128]{1,2,0:T(8,128)S(1)} collective-permute-done((f32[2,128,128]{1,2,0:T(8,128)S(1)}, f32[2,128,128]{1,2,0:T(8,128)S(1)}, u32[]{:S(2)}, u32[]{:S(2)}) %collective-permute-start.7) | collective-permute-done | bytes 131104 | tf_op jit(solution)/shard_map/ppermute | solution.py:32
  40.3 2.8 %collective-permute-start.8 = (f32[2,128,128]{1,2,0:T(8,128)S(1)}, f32[2,128,128]{1,2,0:T(8,128)}, u32[]{:S(2)}, u32[]{:S(2)}) collective-permute-start(f32[2,128,128]{1,2,0:T(8,128)S(1)} %add.537), channel_id=1, source_target_pairs={{0,8},{4,12},{8,0},{12,4},{16,24},{20,28},{24,16},{28,20},{1,9},{5... | collective-permute-start | bytes 393224 | tf_op jit(solution)/shard_map/ppermute | solution.py:32
  43.1 2.4 %fusion.3 = f32[2,128,512]{2,1,0:T(8,128)} fusion(bf16[512,2,128]{0,2,1:T(8,128)(2,1)S(1)} %bitcast.185, f32[2,512,512]{2,1,0:T(8,128)S(1)} %add_multiply_fusion, bf16[512,256]{1,0:T(8,128)(2,1)} %param.14, bf16[512,256]{1,0:T(8,128)(2,1)} %param.15), kind=kOutput, calls=%fused_computation.8 | convolution fusion | flops 269484032 | bytes 3407872 | tf_op jit(solution)/shard_map/hts,thv->shv/dot_general | solution.py:83
  45.5 2.5 %collective-permute-done.5 = f32[2,128,128]{1,2,0:T(8,128)} collective-permute-done((f32[2,128,128]{1,2,0:T(8,128)}, f32[2,128,128]{1,2,0:T(8,128)}, u32[]{:S(2)}, u32[]{:S(2)}) %collective-permute-start.5) | collective-permute-done | bytes 131104 | tf_op jit(solution)/shard_map/ppermute | solution.py:32
  48.0 1.4 %collective-permute-done.8 = f32[2,128,128]{1,2,0:T(8,128)} collective-permute-done((f32[2,128,128]{1,2,0:T(8,128)S(1)}, f32[2,128,128]{1,2,0:T(8,128)}, u32[]{:S(2)}, u32[]{:S(2)}) %collective-permute-start.8) | collective-permute-done | bytes 131104 | tf_op jit(solution)/shard_map/ppermute | solution.py:32
  49.4 1.2 %add_convert_fusion = (bf16[2,128,128]{1,2,0:T(8,128)(2,1)S(1)}, bf16[1,2,128,128]{2,3,1,0:T(8,128)(2,1)S(1)}, bf16[1,2,128,128]{2,3,1,0:T(8,128)(2,1)S(1)}, bf16[1,2,128,128]{2,3,1,0:T(8,128)(2,1)S(1)}) fusion(f32[2,128,128]{1,2,0:T(8,128)} %collective-permute-done.3, f32[]{:T(128)S(6)} %sub.23, f32[]{:T(128)S(6)} %sub.22, f32[]{:T(128)S(6)} %sub.21, ...), kind=kLoop, calls=%fused_computation.89 | loop fusion | flops 458752 | bytes 917528 | tf_op jit(solution)/shard_map/convert_element_type | solution.py:115
  51.5 0.8 %copy.56 = bf16[512,256]{1,0:T(8,128)(2,1)} copy(bf16[512,256]{0,1:T(8,128)(2,1)S(1)} %bitcast.189) | data formatting | bytes 524288
  52.6 1.3 %fusion.7 = bf16[512,2,128]{0,2,1:T(8,128)(2,1)S(1)} fusion(f32[512,2,128]{0,2,1:T(8,128)S(1)} %convolution_bitcast_fusion.1, bf16[2,512,512]{2,1,0:T(8,128)(2,1)S(1)} %copy-done.1, bf16[512,256]{1,0:T(8,128)(2,1)} %param.14), kind=kOutput, calls=%fused_computation.16 | convolution fusion | flops 134479872 | bytes 2097152 | tf_op jit(solution)/shard_map/hts,thk->shk/dot_general | solution.py:80
  53.9 0.8 %copy.57 = bf16[512,256]{1,0:T(8,128)(2,1)} copy(bf16[512,256]{0,1:T(8,128)(2,1)S(1)} %bitcast.188) | data formatting | bytes 524288
  55.0 0.8 %copy.58 = bf16[512,256]{1,0:T(8,128)(2,1)} copy(bf16[512,256]{0,1:T(8,128)(2,1)S(1)} %bitcast.187) | data formatting | bytes 524288
  (65 shorter events, 5.4 us)
Async XLA Ops:
  0.6 21.8 %copy-start = (bf16[256,2048]{1,0:T(8,128)(2,1)S(1)}, bf16[256,2048]{1,0:T(8,128)(2,1)}, u32[]{:S(2)}) copy-start(bf16[256,2048]{1,0:T(8,128)(2,1)} %param.18) | copy-start | bytes 3145732
  0.6 6.1 %copy-start.15 = (s32[512,40]{0,1:T(8,128)S(1)}, s32[512,40]{0,1:T(8,128)}, u32[]{:S(2)}) copy-start(s32[512,40]{0,1:T(8,128)} %param.19) | copy-start | bytes 245764
  0.7 12.6 %collective-permute-start = (bf16[512,512]{1,0:T(8,128)(2,1)}, bf16[512,512]{1,0:T(8,128)(2,1)S(1)}, u32[]{:S(2)}, u32[]{:S(2)}) collective-permute-start(bf16[512,512]{1,0:T(8,128)(2,1)} %param.17), channel_id=1, source_target_pairs={{0,1},{1,2},{2,3},{3,0},{4,5},{5,6},{6,7},{7,4},{8,9},{9,10},{10,1... | collective-permute-start | bytes 1572872 | tf_op jit(solution)/shard_map/ppermute | solution.py:17
  1.2 20.9 %collective-permute-start.2 = (bf16[512,512]{1,0:T(8,128)(2,1)}, bf16[512,512]{1,0:T(8,128)(2,1)S(1)}, u32[]{:S(2)}, u32[]{:S(2)}) collective-permute-start(bf16[512,512]{1,0:T(8,128)(2,1)} %param.17), channel_id=1, source_target_pairs={{0,3},{1,0},{2,1},{3,2},{4,7},{5,4},{6,5},{7,6},{8,11},{9,8},{10,9... | collective-permute-start | bytes 1572872 | tf_op jit(solution)/shard_map/ppermute | solution.py:20
  13.2 8.6 %collective-permute-start.1 = (bf16[512,512]{1,0:T(8,128)(2,1)S(1)}, bf16[512,512]{1,0:T(8,128)(2,1)S(1)}, u32[]{:S(2)}, u32[]{:S(2)}) collective-permute-start(bf16[512,512]{1,0:T(8,128)(2,1)S(1)} %collective-permute-done), channel_id=1, source_target_pairs={{0,1},{1,2},{2,3},{3,0},{4,5},{5,6},{6,7},{7,4},{8,9},{9,10},{10,1... | collective-permute-start | bytes 1572872 | tf_op jit(solution)/shard_map/ppermute | solution.py:17
  16.2 5.7 %copy-start.10 = (bf16[512,512]{1,0:T(8,128)(2,1)S(1)}, bf16[512,512]{1,0:T(8,128)(2,1)}, u32[]{:S(2)}) copy-start(bf16[512,512]{1,0:T(8,128)(2,1)} %param.17) | copy-start | bytes 1572868
  22.5 1.3 %copy-start.8 = (bf16[512,256]{1,0:T(8,128)(2,1)S(1)}, bf16[512,256]{1,0:T(8,128)(2,1)}, u32[]{:S(2)}) copy-start(bf16[512,256]{1,0:T(8,128)(2,1)} %param.15) | copy-start | bytes 786436
  22.5 1.3 %copy-start.12 = (bf16[512,256]{1,0:T(8,128)(2,1)S(1)}, bf16[512,256]{1,0:T(8,128)(2,1)}, u32[]{:S(2)}) copy-start(bf16[512,256]{1,0:T(8,128)(2,1)} %param.16) | copy-start | bytes 786436
  22.5 5.4 %copy-start.5 = (f32[512,512]{1,0:T(8,128)S(1)}, f32[512,512]{1,0:T(8,128)}, u32[]{:S(2)}) copy-start(f32[512,512]{1,0:T(8,128)} %get-tuple-element.83) | copy-start | bytes 3145732
  22.5 5.4 %copy-start.6 = (f32[512,512]{1,0:T(8,128)S(1)}, f32[512,512]{1,0:T(8,128)}, u32[]{:S(2)}) copy-start(f32[512,512]{1,0:T(8,128)} %get-tuple-element.80) | copy-start | bytes 3145732
  22.5 5.4 %copy-start.7 = (f32[512,512]{1,0:T(8,128)S(1)}, f32[512,512]{1,0:T(8,128)}, u32[]{:S(2)}) copy-start(f32[512,512]{1,0:T(8,128)} %get-tuple-element.81) | copy-start | bytes 3145732
  23.3 4.6 %copy-start.2 = (f32[512,512]{1,0:T(8,128)S(1)}, f32[512,512]{1,0:T(8,128)}, u32[]{:S(2)}) copy-start(f32[512,512]{1,0:T(8,128)} %get-tuple-element.84) | copy-start | bytes 3145732
  23.3 4.6 %copy-start.3 = (f32[512,512]{1,0:T(8,128)S(1)}, f32[512,512]{1,0:T(8,128)}, u32[]{:S(2)}) copy-start(f32[512,512]{1,0:T(8,128)} %get-tuple-element.85) | copy-start | bytes 3145732
  23.3 4.6 %copy-start.4 = (f32[512,512]{1,0:T(8,128)S(1)}, f32[512,512]{1,0:T(8,128)}, u32[]{:S(2)}) copy-start(f32[512,512]{1,0:T(8,128)} %get-tuple-element.82) | copy-start | bytes 3145732
  24.8 7.6 %collective-permute-start.6 = (f32[2,128,128]{1,2,0:T(8,128)S(1)}, f32[2,128,128]{1,2,0:T(8,128)S(1)}, u32[]{:S(2)}, u32[]{:S(2)}) collective-permute-start(f32[2,128,128]{1,2,0:T(8,128)S(1)} %get-tuple-element.50), channel_id=1, source_target_pairs={{0,16},{4,20},{8,24},{12,28},{16,0},{20,4},{24,8},{28,12},{1,17},{... | collective-permute-start | bytes 393224 | tf_op jit(solution)/shard_map/ppermute | solution.py:32
  29.8 9.6 %collective-permute-start.4 = (f32[2,128,128]{1,2,0:T(8,128)S(1)}, f32[2,128,128]{1,2,0:T(8,128)}, u32[]{:S(2)}, u32[]{:S(2)}) collective-permute-start(f32[2,128,128]{1,2,0:T(8,128)S(1)} %get-tuple-element.51), channel_id=1, source_target_pairs={{0,8},{4,12},{8,0},{12,4},{16,24},{20,28},{24,16},{28,20},{1,9},{5... | collective-permute-start | bytes 393224 | tf_op jit(solution)/shard_map/ppermute | solution.py:32
  32.4 7.9 %collective-permute-start.7 = (f32[2,128,128]{1,2,0:T(8,128)S(1)}, f32[2,128,128]{1,2,0:T(8,128)S(1)}, u32[]{:S(2)}, u32[]{:S(2)}) collective-permute-start(f32[2,128,128]{1,2,0:T(8,128)S(1)} %collective-permute-done.6), channel_id=1, source_target_pairs={{0,4},{4,0},{8,12},{12,8},{16,20},{20,16},{24,28},{28,24},{1,5},{5... | collective-permute-start | bytes 393224 | tf_op jit(solution)/shard_map/ppermute | solution.py:32
  35.5 10.0 %collective-permute-start.3 = (f32[2,128,128]{1,2,0:T(8,128)}, f32[2,128,128]{1,2,0:T(8,128)}, u32[]{:S(2)}, u32[]{:S(2)}) collective-permute-start(f32[2,128,128]{1,2,0:T(8,128)} %get-tuple-element.49), channel_id=1, source_target_pairs={{0,4},{4,0},{8,12},{12,8},{16,20},{20,16},{24,28},{28,24},{1,5},{5... | collective-permute-start | bytes 393224 | tf_op jit(solution)/shard_map/ppermute | solution.py:32
  39.4 8.7 %collective-permute-start.5 = (f32[2,128,128]{1,2,0:T(8,128)}, f32[2,128,128]{1,2,0:T(8,128)}, u32[]{:S(2)}, u32[]{:S(2)}) collective-permute-start(f32[2,128,128]{1,2,0:T(8,128)} %collective-permute-done.4), channel_id=1, source_target_pairs={{0,4},{4,0},{8,12},{12,8},{16,20},{20,16},{24,28},{28,24},{1,5},{5... | collective-permute-start | bytes 393224 | tf_op jit(solution)/shard_map/ppermute | solution.py:32
  40.3 9.1 %collective-permute-start.8 = (f32[2,128,128]{1,2,0:T(8,128)S(1)}, f32[2,128,128]{1,2,0:T(8,128)}, u32[]{:S(2)}, u32[]{:S(2)}) collective-permute-start(f32[2,128,128]{1,2,0:T(8,128)S(1)} %add.537), channel_id=1, source_target_pairs={{0,8},{4,12},{8,0},{12,4},{16,24},{20,28},{24,16},{28,20},{1,9},{5... | collective-permute-start | bytes 393224 | tf_op jit(solution)/shard_map/ppermute | solution.py:32
  45.5 5.5 %copy-start.1 = (bf16[2,512,512]{2,1,0:T(8,128)(2,1)S(1)}, bf16[2,512,512]{2,1,0:T(8,128)(2,1)}, u32[]{:S(2)}) copy-start(bf16[2,512,512]{2,1,0:T(8,128)(2,1)} %multiply_convert_fusion.1) | copy-start | bytes 3145732
  45.5 5.5 %copy-start.9 = (bf16[512,256]{1,0:T(8,128)(2,1)S(1)}, bf16[512,256]{1,0:T(8,128)(2,1)}, u32[]{:S(2)}) copy-start(bf16[512,256]{1,0:T(8,128)(2,1)} %param.15) | copy-start | bytes 786436
  50.6 1.8 %copy-start.13 = (bf16[512,256]{1,0:T(8,128)(2,1)S(1)}, bf16[512,256]{1,0:T(8,128)(2,1)}, u32[]{:S(2)}) copy-start(bf16[512,256]{1,0:T(8,128)(2,1)} %param.16) | copy-start | bytes 786436
  51.5 3.3 %copy-start.11 = (f32[2,128,512]{2,1,0:T(8,128)S(1)}, f32[2,128,512]{2,1,0:T(8,128)}, u32[]{:S(2)}) copy-start(f32[2,128,512]{2,1,0:T(8,128)} %fusion.3) | copy-start | bytes 1572868
  (1 other events, 1.0 us)
